TPU v7x, 128 devices: a whole 4x4x4 slice. The times are simulated.
128 devices in a mesh: ctx: 32 (over x, z, y_lo), fsdp: 4 (over y_hi, core).
Axes of the slice: x: 4, y: 4 (y_hi: 2, y_lo: 2; y = y_hi * 2 + y_lo), z: 4, core: 2. Of those that a mesh axis runs over, the one named last changes fastest.
Arguments:
- x_cur: bfloat16 [4, 8192, 2048], P('fsdp', 'ctx'), may hold values from -6 to 6
- x_next: bfloat16 [4, 8192, 2048], P('fsdp', 'ctx'), may hold values from -6 to 6
- cot_cur: bfloat16 [4, 8192, 2048], P('fsdp', 'ctx'), may hold values from -6 to 6
- cot_next: bfloat16 [4, 8192, 2048], P('fsdp', 'ctx'), may hold values from -6 to 6
- w_q: bfloat16 [2048, 1024], P('fsdp')
- w_kv: bfloat16 [2048, 512], P('fsdp')
- w_out: bfloat16 [2048, 1024], P('fsdp'), may hold values from -0.1875 to 0.1875
Outputs:
- x_prev: bfloat16 [4, 8192, 2048], P('fsdp', 'ctx')
- grad_cur: bfloat16 [4, 8192, 2048], P('fsdp', 'ctx')
- grad_weights: float32 [2048, 2560], P(('ctx', 'fsdp'))
All inputs are finite; a program needn't handle non-finite values.
Results may differ from a plain program's by a relative error of at most 0.015.
The roundings to bfloat16 on the way count: a program that leaves them out, or rounds other values in their place, can miss the bound.
Values may be sent and summed in bfloat16 or wider, within the bound.
No kernel may reach another device: no remote copies, remote signals or barrier semaphores. Data moves between devices by JAX's collectives and lax.ppermute only.
A program may use at most 192 MiB of HBM per device.

v0:
```python
import math
import jax
import jax.numpy as jnp
from jax import lax
from jax.sharding import Mesh
from jax.sharding import PartitionSpec as P

QUERY_HEADS = 8
KEY_VALUE_HEADS = 2
HEAD_SIZE = 128
WINDOW_TOKENS = 1024
EPS = 1e-05
CTX = ("x", "z", "yl")
FSDP = ("yh", "c")
CHIPS = ("x", "z", "yl", "yh")


def from_behind(value, axis, steps):
    count = lax.axis_size(axis)
    leading, last = (max(0, -steps), min(count, count - steps))
    return lax.ppermute(value, axis, [(source, source + steps) for source in range(leading, last)])


def swap_cores(value):
    return lax.ppermute(value, "c", [(0, 1), (1, 0)])


def normalize(rows):
    values = rows.astype(jnp.float32)
    inv_rms = lax.rsqrt(jnp.mean(values * values, axis=-1, keepdims=True) + EPS)
    return (values * inv_rms, inv_rms)


def head_block(items, allowed):
    quer3, keys2, vals2, grad3 = items
    scale = 1.0 / math.sqrt(HEAD_SIZE)
    scores = jnp.einsum("imd,jd->mij", quer3, keys2, preferred_element_type=jnp.float32) * scale
    scores = jnp.where(allowed[None], scores, -jnp.inf)
    top = jnp.max(scores, axis=-1, keepdims=True)
    expo = jnp.exp(scores - top)
    probs = expo / jnp.sum(expo, axis=-1, keepdims=True)
    probs_low = probs.astype(jnp.bfloat16)
    attended = jnp.einsum("mij,jd->imd", probs_low, vals2, preferred_element_type=jnp.float32)
    grad_probs = jnp.einsum("imd,jd->mij", grad3, vals2, preferred_element_type=jnp.float32)
    delta = jnp.einsum("imd,imd->mi", grad3.astype(jnp.float32), attended)
    grad_scores = (probs * (grad_probs - delta[..., None]) * scale).astype(jnp.bfloat16)
    grad_query = jnp.einsum("mij,jd->imd", grad_scores, keys2, preferred_element_type=jnp.float32)
    key_gradient = jnp.einsum("mij,imd->jd", grad_scores, quer3, preferred_element_type=jnp.float32)
    value_gradient = jnp.einsum("mij,imd->jd", probs_low, grad3, preferred_element_type=jnp.float32)
    return (
        attended.astype(jnp.bfloat16),
        grad_query.astype(jnp.bfloat16),
        key_gradient.astype(jnp.bfloat16),
        value_gradient.astype(jnp.bfloat16),
    )


def window_block(query_rows, key_value_pairs, output_gradient, base):
    window_extent = key_value_pairs.shape[0]
    element_count = query_rows.shape[0]
    query_group = QUERY_HEADS // KEY_VALUE_HEADS
    query_pos = base + jnp.arange(element_count, dtype=jnp.int32)
    key_pos = base - WINDOW_TOKENS + jnp.arange(window_extent, dtype=jnp.int32)
    offset = query_pos[:, None] - key_pos[None, :]
    allowed = (offset >= 0) & (offset < WINDOW_TOKENS) & (key_pos[None, :] >= 0)
    query_grouped = query_rows.reshape(
        element_count, KEY_VALUE_HEADS, query_group, HEAD_SIZE
    ).transpose(1, 0, 2, 3)
    gradient_grouped = output_gradient.reshape(
        element_count, KEY_VALUE_HEADS, query_group, HEAD_SIZE
    ).transpose(1, 0, 2, 3)
    key_tensor = (
        key_value_pairs[:, : KEY_VALUE_HEADS * HEAD_SIZE]
        .reshape(window_extent, KEY_VALUE_HEADS, HEAD_SIZE)
        .transpose(1, 0, 2)
    )
    value_tensor = (
        key_value_pairs[:, KEY_VALUE_HEADS * HEAD_SIZE :]
        .reshape(window_extent, KEY_VALUE_HEADS, HEAD_SIZE)
        .transpose(1, 0, 2)
    )

    def per_head(items):
        return head_block(items, allowed)

    attended, grad_query, key_gradient, value_gradient = lax.map(
        per_head, (query_grouped, key_tensor, value_tensor, gradient_grouped)
    )
    attended = attended.transpose(1, 0, 2, 3).reshape(element_count, QUERY_HEADS * HEAD_SIZE)
    grad_query = grad_query.transpose(1, 0, 2, 3).reshape(element_count, QUERY_HEADS * HEAD_SIZE)
    key_gradient = key_gradient.transpose(1, 0, 2).reshape(
        window_extent, KEY_VALUE_HEADS * HEAD_SIZE
    )
    value_gradient = value_gradient.transpose(1, 0, 2).reshape(
        window_extent, KEY_VALUE_HEADS * HEAD_SIZE
    )
    value_partial_sum = jnp.concatenate([key_gradient, value_gradient], 1)
    return (attended, grad_query, value_partial_sum)


def shards(x_cur, x_next, cot_cur, cot_next, w_q, w_kv, w_out):
    full_q, full_kv, full_out = (
        lax.all_gather(w_q, FSDP, axis=0, tiled=True),
        lax.all_gather(w_kv, FSDP, axis=0, tiled=True),
        lax.all_gather(w_out, FSDP, axis=0, tiled=True),
    )
    seq_count, shard, width = x_cur.shape
    base = lax.axis_index(CTX) * shard
    preds = WINDOW_TOKENS // shard
    normed, inv_rms = normalize(x_cur)
    hidden = normed.astype(jnp.bfloat16)
    query_rows = jnp.einsum(
        "sid,dc->sic", hidden, full_q, preferred_element_type=jnp.float32
    ).astype(jnp.bfloat16)
    key_value_pairs = jnp.einsum(
        "sid,dc->sic", hidden, full_kv, preferred_element_type=jnp.float32
    ).astype(jnp.bfloat16)
    grad_attn = (
        2.0 * jnp.einsum("sid,dc->sic", cot_next, full_out, preferred_element_type=jnp.float32)
    ).astype(jnp.bfloat16)
    earlier = []
    for hop in range(1, preds + 1):
        earlier.append(from_behind(key_value_pairs, CTX, hop))
    window_keys = jnp.concatenate(earlier[::-1] + [key_value_pairs], axis=1)

    def per_sequence(items):
        q_rows, kv_rows, g_rows = items
        return window_block(q_rows, kv_rows, g_rows, base)

    attended, grad_query, value_partial_sum = lax.map(
        per_sequence, (query_rows, window_keys, grad_attn)
    )
    owned = value_partial_sum[:, WINDOW_TOKENS:].astype(jnp.float32)
    for hop in range(1, preds + 1):
        piece = value_partial_sum[
            :, WINDOW_TOKENS - hop * shard : WINDOW_TOKENS - (hop - 1) * shard
        ]
        owned = owned + from_behind(piece, CTX, -hop).astype(jnp.float32)
    grad_kv = owned.astype(jnp.bfloat16)
    layer_out = jnp.einsum("sic,dc->sid", attended, full_out, preferred_element_type=jnp.float32)
    x_prev = (x_next.astype(jnp.float32) - 2.0 * layer_out).astype(jnp.bfloat16)
    grad_hidden = jnp.einsum("sic,dc->sid", grad_query, full_q, preferred_element_type=jnp.float32)
    grad_hidden = grad_hidden + jnp.einsum(
        "sic,dc->sid", grad_kv, full_kv, preferred_element_type=jnp.float32
    )
    grad_x = inv_rms * (
        grad_hidden - normed * jnp.mean(grad_hidden * normed, axis=-1, keepdims=True)
    )
    grad_cur = (cot_cur.astype(jnp.float32) + grad_x).astype(jnp.bfloat16)
    core = lax.axis_index("c")
    token_total = seq_count * shard * lax.axis_size(CTX) * lax.axis_size(FSDP)
    rows_in = hidden.reshape(seq_count * shard, width)
    rows_out = cot_next.reshape(seq_count * shard, width)
    both_in = jnp.concatenate([rows_in, swap_cores(rows_in)], axis=0)
    both_out = jnp.concatenate([rows_out, swap_cores(rows_out)], axis=0)

    def halves(rows):
        rows = rows.reshape(seq_count * shard, -1)
        half = rows.shape[1] // 2
        first = core == 0
        return (
            jnp.where(first, rows[:, :half], rows[:, half:]),
            jnp.where(first, rows[:, half:], rows[:, :half]),
        )

    kept, sent = zip(halves(grad_query), halves(grad_kv), halves(attended))
    kept = jnp.concatenate(kept, axis=1)
    arrived = swap_cores(jnp.concatenate(sent, axis=1))
    split = grad_query.shape[-1] // 2 + grad_kv.shape[-1] // 2
    left = jnp.concatenate([kept, arrived], axis=0)
    contract_rows = (((0,), (0,)), ((), ()))
    term_in = lax.dot_general(
        both_in, left[:, :split], contract_rows, preferred_element_type=jnp.float32
    )
    term_out = 2.0 * lax.dot_general(
        both_out, left[:, split:], contract_rows, preferred_element_type=jnp.float32
    )
    terms = jnp.concatenate([term_in, term_out], axis=1).astype(jnp.bfloat16)
    chips = lax.axis_size(CHIPS)
    terms = terms.reshape(chips, width // chips, -1)
    terms = lax.all_to_all(terms, CHIPS, 0, 0)
    summed = jnp.sum(terms.astype(jnp.float32), axis=0) * (1.0 / math.sqrt(token_total))
    mine = summed.shape[0] // 2
    upper = jnp.where(core == 0, summed[:mine], summed[mine:])
    lower = swap_cores(jnp.where(core == 0, summed[mine:], summed[:mine]))
    zero = jnp.where(core == 0, upper, lower)
    one = jnp.where(core == 0, lower, upper)
    q_half = grad_query.shape[-1] // 2
    grad_weights = jnp.concatenate(
        [
            zero[:, :q_half],
            one[:, :q_half],
            zero[:, q_half:split],
            one[:, q_half:split],
            zero[:, split:],
            one[:, split:],
        ],
        axis=1,
    )
    return (x_prev, grad_cur, grad_weights)


def solution(mesh):
    mesh = Mesh(mesh.devices.reshape(4, 4, 2, 2, 2), CTX + FSDP)
    in_specs = (
        P(FSDP, CTX, None),
        P(FSDP, CTX, None),
        P(FSDP, CTX, None),
        P(FSDP, CTX, None),
        P(FSDP, None),
        P(FSDP, None),
        P(FSDP, None),
    )
    out_specs = (P(FSDP, CTX, None), P(FSDP, CTX, None), P(CTX + FSDP, None))
    return jax.shard_map(shards, mesh=mesh, in_specs=in_specs, out_specs=out_specs, check_vma=False)
```

profile of v0, /device:TPU:71, one launch (start us, length us, event | category | flops | bytes accessed | tf_op | source)
XLA Modules:
  0.0 315.3 jit_solution(6684000862140531037)
XLA Ops:
  10.7 27.6 %all-gather.4.cloned.1.call-done = bf16[2048,512]{1,0:T(8,128)(2,1)} async-done(((bf16[512,512]{1,0:T(8,128)(2,1)}), bf16[2048,512]{1,0:T(8,128)(2,1)}) %all-gather.4.cloned.1.call-update) | async-done | bytes 2097168 | tf_op jit(solution)/shard_map/all_gather | solution.py:104
  41.9 2.9 collective-permute-start.1
  48.7 9.1 %collective-permute-done = bf16[1,256,512]{2,1,0:T(8,128)(2,1)S(1)} collective-permute-done((bf16[1,256,512]{2,1,0:T(8,128)(2,1)S(1)}, bf16[1,256,512]{2,1,0:T(8,128)(2,1)S(1)}, u32[]{:S(2)}, u32[]{:S(2)}) %collective-permute-start) | collective-permute-done | bytes 262176 | tf_op jit(solution)/shard_map/ppermute | solution.py:21
  57.9 11.3 %collective-permute-done.2 = bf16[1,256,512]{2,1,0:T(8,128)(2,1)S(1)} collective-permute-done((bf16[1,256,512]{2,1,0:T(8,128)(2,1)S(1)}, bf16[1,256,512]{2,1,0:T(8,128)(2,1)S(1)}, u32[]{:S(2)}, u32[]{:S(2)}) %collective-permute-start.2) | collective-permute-done | bytes 262176 | tf_op jit(solution)/shard_map/ppermute | solution.py:21
  71.4 14.4 %all-gather.8.cloned.1.call-done = bf16[2048,1024]{1,0:T(8,128)(2,1)} async-done(((bf16[512,1024]{1,0:T(8,128)(2,1)}), bf16[2048,1024]{1,0:T(8,128)(2,1)}) %all-gather.8.cloned.1.call-update) | async-done | bytes 4194320 | tf_op jit(solution)/shard_map/all_gather | solution.py:105
  85.8 3.8 %fusion.76 = bf16[256,1024]{1,0:T(8,128)(2,1)S(1)} fusion(bf16[2048,1024]{1,0:T(8,128)(2,1)} %all-gather.8.cloned.1.call-done, bf16[1,256,2048]{2,1,0:T(8,128)(2,1)} %param.12), kind=kOutput, calls=%fused_computation.93 | convolution fusion | flops 1074266112 | bytes 5767168 | tf_op jit(solution)/shard_map/sid,dc->sic/dot_general | solution.py:119
  90.0 37.9 %all-gather.6.cloned.1.call-done = bf16[2048,1024]{1,0:T(8,128)(2,1)} async-done(((bf16[512,1024]{1,0:T(8,128)(2,1)}), bf16[2048,1024]{1,0:T(8,128)(2,1)}) %all-gather.6.cloned.1.call-update) | async-done | bytes 4194320 | tf_op jit(solution)/shard_map/all_gather | solution.py:103
  127.9 3.4 %convolution_convert_fusion.2 = bf16[256,1024]{1,0:T(8,128)(2,1)S(1)} fusion(bf16[256,2048]{1,0:T(8,128)(2,1)S(1)} %fusion.78, bf16[2048,1024]{1,0:T(8,128)(2,1)} %all-gather.6.cloned.1.call-done), kind=kOutput, calls=%fused_computation.94 | convolution fusion | flops 1074003968 | bytes 5767168 | tf_op jit(solution)/shard_map/sid,dc->sic/dot_general | solution.py:112
  132.9 46.7 %while.29 = (s32[]{:T(128)}, bf16[2,256,4,128]{1,3,2,0:T(8,128)(2,1)}, bf16[2,256,4,128]{1,3,2,0:T(8,128)(2,1)}, bf16[2,1280,128]{1,2,0:T(8,128)(2,1)}, bf16[2,1...) while((s32[]{:T(128)}, ...), condition=%wide.region_4.5_spmd.clone, body=%wide.region_1.4_spmd.clone.sunk | while | flops 2030305536 | bytes 57441732 | solution.py:86
  135.0 5.2 %exponential_reduce_fusion.2 = (f32[4,256]{1,0:T(4,128)S(1)}, f32[4,256,1280]{1,2,0:T(8,128)}) fusion(pred[256,1280]{0,1:T(8,128)(4,1)S(1)} %fusion.142, bf16[2,1280,128]{2,1,0:T(8,128)(2,1)} %get-tuple-element.280, s32[]{:T(128)S(6)} %copy.69, bf16[2,256,4,128]{3,1,2,0:T(8,128)(2,1)} %get-tuple-element.281), kind=kOutput, calls=%fused_computation.9.clone.1 | convolution fusion | flops 340788480 | bytes 6165504 | tf_op jit(solution)/shard_map/while/body/eval_jaxpr/while/body/eval_jaxpr/sub | solution.py:40
  140.2 4.0 %fusion.143 = bf16[4,256,1280]{1,2,0:T(8,128)(2,1)S(1)} fusion(f32[4,256]{1,0:T(4,128)S(1)} %get-tuple-element.242, f32[4,256,1280]{1,2,0:T(8,128)} %get-tuple-element.243), kind=kLoop, calls=%fused_computation.18.clone.1 | loop fusion | flops 2621440 | bytes 7868416 | tf_op jit(solution)/shard_map/while/body/eval_jaxpr/while/body/eval_jaxpr/convert_element_type | solution.py:42
  148.4 2.5 fusion.146
  158.4 5.2 %exponential_reduce_fusion.2 = (f32[4,256]{1,0:T(4,128)S(1)}, f32[4,256,1280]{1,2,0:T(8,128)}) fusion(pred[256,1280]{0,1:T(8,128)(4,1)S(1)} %fusion.142, bf16[2,1280,128]{2,1,0:T(8,128)(2,1)} %get-tuple-element.280, s32[]{:T(128)S(6)} %copy.69, bf16[2,256,4,128]{3,1,2,0:T(8,128)(2,1)} %get-tuple-element.281), kind=kOutput, calls=%fused_computation.9.clone.1 | convolution fusion | flops 340788480 | bytes 6165504 | tf_op jit(solution)/shard_map/while/body/eval_jaxpr/while/body/eval_jaxpr/sub | solution.py:40
  163.6 4.0 %fusion.143 = bf16[4,256,1280]{1,2,0:T(8,128)(2,1)S(1)} fusion(f32[4,256]{1,0:T(4,128)S(1)} %get-tuple-element.242, f32[4,256,1280]{1,2,0:T(8,128)} %get-tuple-element.243), kind=kLoop, calls=%fused_computation.18.clone.1 | loop fusion | flops 2621440 | bytes 7868416 | tf_op jit(solution)/shard_map/while/body/eval_jaxpr/while/body/eval_jaxpr/convert_element_type | solution.py:42
  183.2 4.8 %collective-permute-start.7 = (bf16[1,256,512]{1,2,0:T(8,128)(2,1)S(1)}, bf16[1,256,512]{1,2,0:T(8,128)(2,1)S(1)}, u32[]{:S(2)}, u32[]{:S(2)}) collective-permute-start(bf16[1,256,512]{1,2,0:T(8,128)(2,1)S(1)} %get-tuple-element.146), channel_id=1, source_target_pairs={{16,0},{20,4},{24,8},{28,12},{32,16},{36,20},{40,24},{44,28},{48,3... | collective-permute-start | bytes 786440 | tf_op jit(solution)/shard_map/ppermute | solution.py:21
  188.0 3.3 %collective-permute-start.6 = (bf16[1,256,512]{1,2,0:T(8,128)(2,1)S(1)}, bf16[1,256,512]{1,2,0:T(8,128)(2,1)S(1)}, u32[]{:S(2)}, u32[]{:S(2)}) collective-permute-start(bf16[1,256,512]{1,2,0:T(8,128)(2,1)S(1)} %get-tuple-element.147), channel_id=1, source_target_pairs={{12,0},{16,4},{20,8},{24,12},{28,16},{32,20},{36,24},{40,28},{44,3... | collective-permute-start | bytes 786440 | tf_op jit(solution)/shard_map/ppermute | solution.py:21
  197.9 6.9 %collective-permute-done.5 = bf16[1,256,512]{1,2,0:T(8,128)(2,1)S(1)} collective-permute-done((bf16[1,256,512]{1,2,0:T(8,128)(2,1)S(1)}, bf16[1,256,512]{1,2,0:T(8,128)(2,1)S(1)}, u32[]{:S(2)}, u32[]{:S(2)}) %collective-permute-start.5) | collective-permute-done | bytes 262176 | tf_op jit(solution)/shard_map/ppermute | solution.py:21
  207.9 2.9 multiply_convert_fusion
  212.8 2.8 pad_maximum_fusion
  215.6 14.9 %all-to-all-start = ((bf16[64,32,1280]{2,1,0:T(8,128)(2,1)}), bf16[64,32,1280]{2,1,0:T(8,128)(2,1)}, u32[]{:S(2)}, u32[]{:S(2)}) async-start(bf16[64,32,1280]{2,1,0:T(8,128)(2,1)} %pad_maximum_fusion), calls=%async_computation | async-start | bytes 10485760 | tf_op jit(solution)/shard_map/all_to_all | solution.py:181
  230.5 3.8 %fusion.96 = f32[256,2048]{1,0:T(8,128)S(1)} fusion(bf16[256,1024]{0,1:T(8,128)(2,1)} %bitcast.15, bf16[2048,1024]{1,0:T(8,128)(2,1)} %all-gather.6.cloned.1.call-done), kind=kOutput, calls=%fused_computation.144 | convolution fusion | flops 1073741824 | bytes 6815744 | tf_op jit(solution)/shard_map/sic,dc->sid/dot_general | solution.py:142
  234.4 3.5 %fusion.63 = bf16[1,256,2048]{2,1,0:T(8,128)(2,1)} fusion(bf16[256,1024]{0,1:T(8,128)(2,1)} %bitcast.12, bf16[2048,1024]{1,0:T(8,128)(2,1)S(1)} %copy-done.7, bf16[1,256,2048]{2,1,0:T(8,128)(2,1)S(1)} %copy-done.8), kind=kOutput, calls=%fused_computation.77 | convolution fusion | flops 1075838976 | bytes 6815744 | tf_op jit(solution)/shard_map/sic,dc->sid/dot_general | solution.py:140
  238.9 62.1 %all-to-all-done = bf16[64,32,1280]{2,1,0:T(8,128)(2,1)} async-done(((bf16[64,32,1280]{2,1,0:T(8,128)(2,1)}), bf16[64,32,1280]{2,1,0:T(8,128)(2,1)}, u32[]{:S(2)}, u32[]{:S(2)}) %all-to-all-start) | async-done | bytes 5242912 | tf_op jit(solution)/shard_map/all_to_all | solution.py:181
  301.0 3.4 %convert_reduce_fusion = f32[32,1280]{1,0:T(8,128)S(1)} fusion(bf16[64,32,1280]{2,1,0:T(8,128)(2,1)} %all-to-all-done), kind=kLoop, calls=%fused_computation.63 | loop fusion | flops 5201920 | bytes 5406720 | tf_op jit(solution)/shard_map/reduce_sum | solution.py:182
  (118 shorter events, 61.5 us)
Async XLA Ops:
  7.2 31.1 %all-gather.4.cloned.1.call-start = ((), (), s32[]{:S(2)}) async-start(), calls=%async_computation.1 | async-start | bytes 2621440 | tf_op jit(solution)/shard_map/all_gather | solution.py:104
  7.9 77.9 %all-gather.8.cloned.1.call-start = ((), (), s32[]{:S(2)}) async-start(), calls=%async_computation.3 | async-start | bytes 5242880 | tf_op jit(solution)/shard_map/all_gather | solution.py:105
  8.7 119.2 %all-gather.6.cloned.1.call-start = ((), (), s32[]{:S(2)}) async-start(), calls=%async_computation.2 | async-start | bytes 5242880 | tf_op jit(solution)/shard_map/all_gather | solution.py:103
  9.4 196.9 %collective-permute-start.10 = (bf16[256,2048]{1,0:T(8,128)(2,1)}, bf16[256,2048]{1,0:T(8,128)(2,1)}, u32[]{:S(2)}, u32[]{:S(2)}) collective-permute-start(bf16[256,2048]{1,0:T(8,128)(2,1)} %bitcast.9), channel_id=1, source_target_pairs={{0,1},{1,0},{2,3},{3,2},{4,5},{5,4},{6,7},{7,6},{8,9},{9,8},{10,11... | collective-permute-start | bytes 3145736 | tf_op jit(solution)/shard_map/ppermute | solution.py:25
  10.7 117.2 %copy-start.4 = (bf16[256,2048]{1,0:T(8,128)(2,1)}, bf16[256,2048]{1,0:T(8,128)(2,1)S(1)}, u32[]{:S(2)}) copy-start(bf16[256,2048]{1,0:T(8,128)(2,1)S(1)} %fusion.78) | copy-start | bytes 3145732
  40.6 17.3 %collective-permute-start = (bf16[1,256,512]{2,1,0:T(8,128)(2,1)S(1)}, bf16[1,256,512]{2,1,0:T(8,128)(2,1)S(1)}, u32[]{:S(2)}, u32[]{:S(2)}) collective-permute-start(bf16[1,256,512]{2,1,0:T(8,128)(2,1)S(1)} %fusion.77), channel_id=1, source_target_pairs={{0,16},{4,20},{8,24},{12,28},{16,32},{20,36},{24,40},{28,44},{32,4... | collective-permute-start | bytes 786440 | tf_op jit(solution)/shard_map/ppermute | solution.py:21
  41.9 16.0 %collective-permute-start.1 = (bf16[1,256,512]{2,1,0:T(8,128)(2,1)S(1)}, bf16[1,256,512]{2,1,0:T(8,128)(2,1)S(1)}, u32[]{:S(2)}, u32[]{:S(2)}) collective-permute-start(bf16[1,256,512]{2,1,0:T(8,128)(2,1)S(1)} %fusion.77), channel_id=1, source_target_pairs={{0,12},{4,16},{8,20},{12,24},{16,28},{20,32},{24,36},{28,40},{32,4... | collective-permute-start | bytes 786440 | tf_op jit(solution)/shard_map/ppermute | solution.py:21
  44.8 24.4 %collective-permute-start.2 = (bf16[1,256,512]{2,1,0:T(8,128)(2,1)S(1)}, bf16[1,256,512]{2,1,0:T(8,128)(2,1)S(1)}, u32[]{:S(2)}, u32[]{:S(2)}) collective-permute-start(bf16[1,256,512]{2,1,0:T(8,128)(2,1)S(1)} %fusion.77), channel_id=1, source_target_pairs={{0,8},{4,12},{8,16},{12,20},{16,24},{20,28},{24,32},{28,36},{32,40... | collective-permute-start | bytes 786440 | tf_op jit(solution)/shard_map/ppermute | solution.py:21
  46.8 22.4 %collective-permute-start.3 = (bf16[1,256,512]{2,1,0:T(8,128)(2,1)S(1)}, bf16[1,256,512]{2,1,0:T(8,128)(2,1)S(1)}, u32[]{:S(2)}, u32[]{:S(2)}) collective-permute-start(bf16[1,256,512]{2,1,0:T(8,128)(2,1)S(1)} %fusion.77), channel_id=1, source_target_pairs={{0,4},{4,8},{8,12},{12,16},{16,20},{20,24},{24,28},{28,32},{32,36}... | collective-permute-start | bytes 786440 | tf_op jit(solution)/shard_map/ppermute | solution.py:21
  140.2 8.2 %slice-start = ((s8[5242880]{0:T(1024)(128)(4,1)}), s8[4194304]{0:T(1024)(128)(4,1)S(1)}, s32[]{:S(2)}) async-start(s8[5242880]{0:T(1024)(128)(4,1)} %bitcast.206), calls=%async_computation.4 | async-start | bytes 8388608 | tf_op jit(solution)/shard_map/while/body/eval_jaxpr/while
  144.2 4.2 %slice-start.1 = ((s8[5242880]{0:T(1024)(128)(4,1)}), s8[1048576]{0:T(1024)(128)(4,1)S(1)}, s32[]{:S(2)}) async-start(s8[5242880]{0:T(1024)(128)(4,1)} %bitcast.206), calls=%async_computation.5 | async-start | bytes 2097152 | tf_op jit(solution)/shard_map/while/body/eval_jaxpr/while
  163.6 8.2 %slice-start = ((s8[5242880]{0:T(1024)(128)(4,1)}), s8[4194304]{0:T(1024)(128)(4,1)S(1)}, s32[]{:S(2)}) async-start(s8[5242880]{0:T(1024)(128)(4,1)} %bitcast.206), calls=%async_computation.4 | async-start | bytes 8388608 | tf_op jit(solution)/shard_map/while/body/eval_jaxpr/while
  167.6 4.2 %slice-start.1 = ((s8[5242880]{0:T(1024)(128)(4,1)}), s8[1048576]{0:T(1024)(128)(4,1)S(1)}, s32[]{:S(2)}) async-start(s8[5242880]{0:T(1024)(128)(4,1)} %bitcast.206), calls=%async_computation.5 | async-start | bytes 2097152 | tf_op jit(solution)/shard_map/while/body/eval_jaxpr/while
  181.1 14.5 %collective-permute-start.4 = (bf16[1,256,512]{1,2,0:T(8,128)(2,1)S(1)}, bf16[1,256,512]{1,2,0:T(8,128)(2,1)S(1)}, u32[]{:S(2)}, u32[]{:S(2)}) collective-permute-start(bf16[1,256,512]{1,2,0:T(8,128)(2,1)S(1)} %get-tuple-element.145), channel_id=1, source_target_pairs={{4,0},{8,4},{12,8},{16,12},{20,16},{24,20},{28,24},{32,28},{36,32}... | collective-permute-start | bytes 786440 | tf_op jit(solution)/shard_map/ppermute | solution.py:21
  183.2 12.4 %collective-permute-start.7 = (bf16[1,256,512]{1,2,0:T(8,128)(2,1)S(1)}, bf16[1,256,512]{1,2,0:T(8,128)(2,1)S(1)}, u32[]{:S(2)}, u32[]{:S(2)}) collective-permute-start(bf16[1,256,512]{1,2,0:T(8,128)(2,1)S(1)} %get-tuple-element.146), channel_id=1, source_target_pairs={{16,0},{20,4},{24,8},{28,12},{32,16},{36,20},{40,24},{44,28},{48,3... | collective-permute-start | bytes 786440 | tf_op jit(solution)/shard_map/ppermute | solution.py:21
  188.0 9.9 %collective-permute-start.6 = (bf16[1,256,512]{1,2,0:T(8,128)(2,1)S(1)}, bf16[1,256,512]{1,2,0:T(8,128)(2,1)S(1)}, u32[]{:S(2)}, u32[]{:S(2)}) collective-permute-start(bf16[1,256,512]{1,2,0:T(8,128)(2,1)S(1)} %get-tuple-element.147), channel_id=1, source_target_pairs={{12,0},{16,4},{20,8},{24,12},{28,16},{32,20},{36,24},{40,28},{44,3... | collective-permute-start | bytes 786440 | tf_op jit(solution)/shard_map/ppermute | solution.py:21
  191.3 13.6 %collective-permute-start.5 = (bf16[1,256,512]{1,2,0:T(8,128)(2,1)S(1)}, bf16[1,256,512]{1,2,0:T(8,128)(2,1)S(1)}, u32[]{:S(2)}, u32[]{:S(2)}) collective-permute-start(bf16[1,256,512]{1,2,0:T(8,128)(2,1)S(1)} %get-tuple-element.148), channel_id=1, source_target_pairs={{8,0},{12,4},{16,8},{20,12},{24,16},{28,20},{32,24},{36,28},{40,32... | collective-permute-start | bytes 786440 | tf_op jit(solution)/shard_map/ppermute | solution.py:21
  194.4 11.8 %copy-start.5 = (bf16[256,2048]{1,0:T(8,128)(2,1)S(1)}, bf16[256,2048]{1,0:T(8,128)(2,1)}, u32[]{:S(2)}) copy-start(bf16[256,2048]{1,0:T(8,128)(2,1)} %copy-done.4) | copy-start | bytes 3145732
  205.1 2.9 collective-permute-start.9
  206.2 4.7 %collective-permute-start.8 = (bf16[256,2048]{1,0:T(8,128)(2,1)S(1)}, bf16[256,2048]{1,0:T(8,128)(2,1)S(1)}, u32[]{:S(2)}, u32[]{:S(2)}) collective-permute-start(bf16[256,2048]{1,0:T(8,128)(2,1)S(1)} %copy-done.5), channel_id=1, source_target_pairs={{0,1},{1,0},{2,3},{3,2},{4,5},{5,4},{6,7},{7,6},{8,9},{9,8},{10,11... | collective-permute-start | bytes 3145736 | tf_op jit(solution)/shard_map/ppermute | solution.py:25
  215.6 85.4 %all-to-all-start = ((bf16[64,32,1280]{2,1,0:T(8,128)(2,1)}), bf16[64,32,1280]{2,1,0:T(8,128)(2,1)}, u32[]{:S(2)}, u32[]{:S(2)}) async-start(bf16[64,32,1280]{2,1,0:T(8,128)(2,1)} %pad_maximum_fusion), calls=%async_computation | async-start | bytes 10485760 | tf_op jit(solution)/shard_map/all_to_all | solution.py:181
  230.5 3.9 %copy-start.8 = (bf16[1,256,2048]{2,1,0:T(8,128)(2,1)S(1)}, bf16[1,256,2048]{2,1,0:T(8,128)(2,1)}, u32[]{:S(2)}) copy-start(bf16[1,256,2048]{2,1,0:T(8,128)(2,1)} %param.10) | copy-start | bytes 3145732
  301.0 5.4 %copy-start.3 = (bf16[1,256,2048]{2,1,0:T(8,128)(2,1)S(1)}, bf16[1,256,2048]{2,1,0:T(8,128)(2,1)}, u32[]{:S(2)}) copy-start(bf16[1,256,2048]{2,1,0:T(8,128)(2,1)} %param.11) | copy-start | bytes 3145732
  304.4 3.6 %collective-permute-start.11 = (f32[16,1280]{1,0:T(8,128)S(1)}, f32[16,1280]{1,0:T(8,128)S(1)}, u32[]{:S(2)}, u32[]{:S(2)}) collective-permute-start(f32[16,1280]{1,0:T(8,128)S(1)} %slice_select_fusion), channel_id=1, source_target_pairs={{0,1},{1,0},{2,3},{3,2},{4,5},{5,4},{6,7},{7,6},{8,9},{9,8},{10,11... | collective-permute-start | bytes 245768 | tf_op jit(solution)/shard_map/ppermute | solution.py:25
  (5 other events, 14.4 us)
Sparse Core Ops, SparseCore 0:
  9.7 28.5 all-gather.3
  39.9 45.8 all-gather.7
  87.5 40.3 all-gather.5
where the time goes:
time: 316 us; the launch traced here: 315 us
  waiting for transfers between devices  175 us (55%)
  matrix products  54.2 us (17%)
  starting transfers between devices  39.3 us (12%)
  other arithmetic  24.2 us (8%)
  between operations  14.2 us (4%)
  local copies, waits for them, and re-layouts  7.93 us (3%)
    all_to_all x1, waiting for transfers between devices, shards(): terms = lax.all_to_all(terms, CHIPS, 0, 0)  62.1 us
    all_gather x1, waiting for transfers between devices, shards(): lax.all_gather(w_q, FSDP, axis=0, tiled=True)  37.9 us
    ppermute x8, waiting for transfers between devices, from_behind(): lax.ppermute(value, axis, [(source, source + steps) for source in range(l...  29.6 us
    all_gather x1, waiting for transfers between devices, shards(): lax.all_gather(w_kv, FSDP, axis=0, tiled=True)  27.6 us
    ppermute x8, starting transfers between devices, from_behind(): lax.ppermute(value, axis, [(source, source + steps) for source in range(l...  20.3 us
    all_to_all x1, starting transfers between devices, shards(): terms = lax.all_to_all(terms, CHIPS, 0, 0)  14.9 us
    all_gather x1, waiting for transfers between devices, shards(): lax.all_gather(w_out, FSDP, axis=0, tiled=True)  14.4 us
    sub x2, matrix products, head_block(): expo = jnp.exp(scores - top)  10.4 us
  transfers between devices with their start and end apart: 16, of which 9 were waited for; matrix products, arithmetic and copies ran while one was open for 25% of the time, Pallas kernels for 0%

commit v1 on v0

--- a/solution.py
+++ b/solution.py
@@ -100,7 +100,7 @@
 
 def shards(x_cur, x_next, cot_cur, cot_next, w_q, w_kv, w_out):
     full_q, full_kv, full_out = (
-        lax.all_gather(w_q, FSDP, axis=0, tiled=True),
+        jnp.concatenate(lax.all_to_all(jnp.stack([w_q] * lax.axis_size(FSDP)), FSDP, 0, 0), axis=0),
         lax.all_gather(w_kv, FSDP, axis=0, tiled=True),
         lax.all_gather(w_out, FSDP, axis=0, tiled=True),
     )

time: 316 us -> 317 us (level)
  waiting for transfers between devices: 175 us -> 151 us
  starting transfers between devices: 39.3 us -> 56.1 us
  local copies, waits for them, and re-layouts: 7.93 us -> 16.4 us
    all_gather x1 -> x0, waiting for transfers between devices: 37.9 us -> none  [shards(): lax.all_gather(w_q, FSDP, axis=0, tiled=True)]
    all_to_all x0 -> x1, waiting for transfers between devices: none -> 28.2 us  [shards(): lax.all_to_all(jnp.stack([w_q] * lax.axis_size(FSDP)), FSDP, 0, 0)]
    all_gather x1, waiting for transfers between devices: 14.4 us -> 2.48 us  [shards(): lax.all_gather(w_out, FSDP, axis=0, tiled=True)]
    all_to_all x1, starting transfers between devices: 14.9 us -> 24.6 us  [shards(): terms = lax.all_to_all(terms, CHIPS, 0, 0)]
    ppermute x8, waiting for transfers between devices: 29.6 us -> 21.6 us  [from_behind(): lax.ppermute(value, axis, [(source, source + steps) for source in range(l...]
    while x10 -> x38, local copies, waits for them, and re-layouts: 0.41 us -> 7.12 us
    all_to_all x0 -> x1, starting transfers between devices: none -> 5.58 us  [shards(): lax.all_to_all(jnp.stack([w_q] * lax.axis_size(FSDP)), FSDP, 0, 0)]
    all_gather x1, waiting for transfers between devices: 27.6 us -> 32.1 us  [shards(): lax.all_gather(w_kv, FSDP, axis=0, tiled=True)]
  transfers between devices with their start and end apart: 16 -> 16, of which waited for: 9 -> 8; matrix products, arithmetic and copies ran while one was open for 25% -> 26% of each run, Pallas kernels for 0% -> 0%
where the time goes in v1:
time: 317 us; the launch traced here: 316 us
  waiting for transfers between devices  151 us (48%)
  starting transfers between devices  56.1 us (18%)
  matrix products  54.2 us (17%)
  other arithmetic  23.7 us (7%)
  local copies, waits for them, and re-layouts  16.4 us (5%)
  between operations  14.5 us (5%)
    all_to_all x1, waiting for transfers between devices, shards(): terms = lax.all_to_all(terms, CHIPS, 0, 0)  63.5 us
    all_gather x1, waiting for transfers between devices, shards(): lax.all_gather(w_kv, FSDP, axis=0, tiled=True)  32.1 us
    all_to_all x1, waiting for transfers between devices, shards(): lax.all_to_all(jnp.stack([w_q] * lax.axis_size(FSDP)), FSDP, 0, 0)  28.2 us
    all_to_all x1, starting transfers between devices, shards(): terms = lax.all_to_all(terms, CHIPS, 0, 0)  24.6 us
    ppermute x8, waiting for transfers between devices, from_behind(): lax.ppermute(value, axis, [(source, source + steps) for source in range(l...  21.6 us
    ppermute x8, starting transfers between devices, from_behind(): lax.ppermute(value, axis, [(source, source + steps) for source in range(l...  21.4 us
    sub x2, matrix products, head_block(): expo = jnp.exp(scores - top)  10.1 us
    dot_general x2, matrix products, head_block(): jnp.einsum('imd,jd->mij', grad3, vals2, preferred_element_type=jnp.float32)  8.12 us
  transfers between devices with their start and end apart: 16, of which 8 were waited for; matrix products, arithmetic and copies ran while one was open for 26% of the time, Pallas kernels for 0%

profile of v1, /device:TPU:71, one launch (start us, length us, event | category | flops | bytes accessed | tf_op | source)
XLA Modules:
  0.0 316.0 jit_solution(1303570515897018591)
XLA Ops:
  11.2 5.6 %all-to-all-start = ((bf16[4,512,1024]{2,1,0:T(8,128)(2,1)}), bf16[4,512,1024]{2,1,0:T(8,128)(2,1)}, u32[]{:S(2)}, u32[]{:S(2)}) async-start(bf16[4,512,1024]{2,1,0:T(8,128)(2,1)} %stack.2), calls=%async_computation | async-start | bytes 8388608 | tf_op jit(solution)/shard_map/all_to_all | solution.py:103
  17.5 32.1 %all-gather.3.cloned.1.call-done = bf16[2048,512]{1,0:T(8,128)(2,1)} async-done(((bf16[512,512]{1,0:T(8,128)(2,1)}), bf16[2048,512]{1,0:T(8,128)(2,1)}) %all-gather.3.cloned.1.call-update) | async-done | bytes 2097168 | tf_op jit(solution)/shard_map/all_gather | solution.py:104
  53.2 2.9 collective-permute-start.1
  60.2 28.2 %all-to-all-done = bf16[4,512,1024]{2,1,0:T(8,128)(2,1)} async-done(((bf16[4,512,1024]{2,1,0:T(8,128)(2,1)}), bf16[4,512,1024]{2,1,0:T(8,128)(2,1)}, u32[]{:S(2)}, u32[]{:S(2)}) %all-to-all-start) | async-done | bytes 4194336 | tf_op jit(solution)/shard_map/all_to_all | solution.py:103
  88.4 3.4 %convolution_convert_fusion.2 = bf16[256,1024]{1,0:T(8,128)(2,1)S(1)} fusion(bf16[256,2048]{1,0:T(8,128)(2,1)S(1)} %fusion.78, bf16[2048,1024]{1,0:T(8,128)(2,1)} %bitcast.8), kind=kOutput, calls=%fused_computation.94 | convolution fusion | flops 1074003968 | bytes 5767168 | tf_op jit(solution)/shard_map/sid,dc->sic/dot_general | solution.py:112
  92.2 4.9 %collective-permute-done.1 = bf16[1,256,512]{2,1,0:T(8,128)(2,1)S(1)} collective-permute-done((bf16[1,256,512]{2,1,0:T(8,128)(2,1)S(1)}, bf16[1,256,512]{2,1,0:T(8,128)(2,1)S(1)}, u32[]{:S(2)}, u32[]{:S(2)}) %collective-permute-start.1) | collective-permute-done | bytes 262176 | tf_op jit(solution)/shard_map/ppermute | solution.py:21
  97.1 11.7 %collective-permute-done.3 = bf16[1,256,512]{2,1,0:T(8,128)(2,1)S(1)} collective-permute-done((bf16[1,256,512]{2,1,0:T(8,128)(2,1)S(1)}, bf16[1,256,512]{2,1,0:T(8,128)(2,1)S(1)}, u32[]{:S(2)}, u32[]{:S(2)}) %collective-permute-start.3) | collective-permute-done | bytes 262176 | tf_op jit(solution)/shard_map/ppermute | solution.py:21
  111.8 4.6 %fusion.76 = bf16[256,1024]{1,0:T(8,128)(2,1)} fusion(bf16[2048,1024]{1,0:T(8,128)(2,1)} %all-gather.5.cloned.1.call-done, bf16[1,256,2048]{2,1,0:T(8,128)(2,1)} %param.12), kind=kOutput, calls=%fused_computation.93 | convolution fusion | flops 1074266112 | bytes 5767168 | tf_op jit(solution)/shard_map/sid,dc->sic/dot_general | solution.py:119
  118.9 55.6 %while.29 = (s32[]{:T(128)}, bf16[2,256,4,128]{1,3,2,0:T(8,128)(2,1)}, bf16[2,256,4,128]{1,3,2,0:T(8,128)(2,1)}, bf16[2,1280,128]{1,2,0:T(8,128)(2,1)}, bf16[2,1...) while((s32[]{:T(128)}, ...), condition=%wide.region_4.5_spmd.clone, body=%wide.region_1.4_spmd.clone.sunk | while | flops 2030305536 | bytes 71074424 | solution.py:86
  119.9 5.0 %exponential_reduce_fusion.2 = (f32[4,256]{1,0:T(4,128)S(1)}, f32[4,256,1280]{1,2,0:T(8,128)}) fusion(pred[256,1280]{0,1:T(8,128)(4,1)S(1)} %fusion.142, bf16[2,1280,128]{2,1,0:T(8,128)(2,1)S(1)} %get-tuple-element.280, s32[]{:T(128)} %get-tuple-element.261, bf16[2,256,4,128]{3,1,2,0:T(8,128)(2,1)} %get-tuple-element.281), kind=kOutput, calls=%fused_computation.9.clone.1 | convolution fusion | flops 340788480 | bytes 6165504 | tf_op jit(solution)/shard_map/while/body/eval_jaxpr/while/body/eval_jaxpr/sub | solution.py:40
  124.9 3.9 %fusion.143 = bf16[4,256,1280]{1,2,0:T(8,128)(2,1)S(1)} fusion(f32[4,256]{1,0:T(4,128)S(1)} %get-tuple-element.242, f32[4,256,1280]{1,2,0:T(8,128)} %get-tuple-element.243), kind=kLoop, calls=%fused_computation.18.clone.1 | loop fusion | flops 2621440 | bytes 7868416 | tf_op jit(solution)/shard_map/while/body/eval_jaxpr/while/body/eval_jaxpr/convert_element_type | solution.py:42
  134.2 4.1 %fusion.146 = bf16[4,256,1280]{1,2,0:T(8,128)(2,1)S(1)} fusion(f32[4,256]{1,0:T(4,128)S(1)} %fusion.145, f32[4,256]{1,0:T(4,128)S(1)} %get-tuple-element.242, f32[4,256,1280]{1,2,0:T(8,128)} %get-tuple-element.243, bf16[2,1280,128]{1,2,0:T(8,128)(2,1)} %copy-done.5, s32[]{:T(128)} %get-tuple-element.261, bf16[2,256,4,128]{3,1,2,0:T(8,128)(2,1)} %get-tuple-element.282), kind=kOutput, calls=%fused_computation.6.clone.1 | convolution fusion | flops 342097920 | bytes 8463360 | tf_op jit(solution)/shard_map/while/body/eval_jaxpr/while/body/eval_jaxpr/imd,jd->mij/dot_general | solution.py:44
  143.7 3.1 fusion.147
  147.7 5.0 %exponential_reduce_fusion.2 = (f32[4,256]{1,0:T(4,128)S(1)}, f32[4,256,1280]{1,2,0:T(8,128)}) fusion(pred[256,1280]{0,1:T(8,128)(4,1)S(1)} %fusion.142, bf16[2,1280,128]{2,1,0:T(8,128)(2,1)S(1)} %get-tuple-element.280, s32[]{:T(128)} %get-tuple-element.261, bf16[2,256,4,128]{3,1,2,0:T(8,128)(2,1)} %get-tuple-element.281), kind=kOutput, calls=%fused_computation.9.clone.1 | convolution fusion | flops 340788480 | bytes 6165504 | tf_op jit(solution)/shard_map/while/body/eval_jaxpr/while/body/eval_jaxpr/sub | solution.py:40
  152.7 3.9 %fusion.143 = bf16[4,256,1280]{1,2,0:T(8,128)(2,1)S(1)} fusion(f32[4,256]{1,0:T(4,128)S(1)} %get-tuple-element.242, f32[4,256,1280]{1,2,0:T(8,128)} %get-tuple-element.243), kind=kLoop, calls=%fused_computation.18.clone.1 | loop fusion | flops 2621440 | bytes 7868416 | tf_op jit(solution)/shard_map/while/body/eval_jaxpr/while/body/eval_jaxpr/convert_element_type | solution.py:42
  162.0 4.1 %fusion.146 = bf16[4,256,1280]{1,2,0:T(8,128)(2,1)S(1)} fusion(f32[4,256]{1,0:T(4,128)S(1)} %fusion.145, f32[4,256]{1,0:T(4,128)S(1)} %get-tuple-element.242, f32[4,256,1280]{1,2,0:T(8,128)} %get-tuple-element.243, bf16[2,1280,128]{1,2,0:T(8,128)(2,1)} %copy-done.5, s32[]{:T(128)} %get-tuple-element.261, bf16[2,256,4,128]{3,1,2,0:T(8,128)(2,1)} %get-tuple-element.282), kind=kOutput, calls=%fused_computation.6.clone.1 | convolution fusion | flops 342097920 | bytes 8463360 | tf_op jit(solution)/shard_map/while/body/eval_jaxpr/while/body/eval_jaxpr/imd,jd->mij/dot_general | solution.py:44
  171.5 3.0 fusion.147
  180.4 7.0 %collective-permute-start.6 = (bf16[1,256,512]{1,2,0:T(8,128)(2,1)S(1)}, bf16[1,256,512]{1,2,0:T(8,128)(2,1)S(1)}, u32[]{:S(2)}, u32[]{:S(2)}) collective-permute-start(bf16[1,256,512]{1,2,0:T(8,128)(2,1)S(1)} %get-tuple-element.147), channel_id=1, source_target_pairs={{12,0},{16,4},{20,8},{24,12},{28,16},{32,20},{36,24},{40,28},{44,3... | collective-permute-start | bytes 786440 | tf_op jit(solution)/shard_map/ppermute | solution.py:21
  189.5 5.1 %collective-permute-done.5 = bf16[1,256,512]{1,2,0:T(8,128)(2,1)S(1)} collective-permute-done((bf16[1,256,512]{1,2,0:T(8,128)(2,1)S(1)}, bf16[1,256,512]{1,2,0:T(8,128)(2,1)S(1)}, u32[]{:S(2)}, u32[]{:S(2)}) %collective-permute-start.5) | collective-permute-done | bytes 262176 | tf_op jit(solution)/shard_map/ppermute | solution.py:21
  198.7 2.9 multiply_convert_fusion
  206.2 24.6 %all-to-all-start.1 = ((bf16[64,32,1280]{2,1,0:T(8,128)(2,1)}), bf16[64,32,1280]{2,1,0:T(8,128)(2,1)}, u32[]{:S(2)}, u32[]{:S(2)}) async-start(bf16[64,32,1280]{2,1,0:T(8,128)(2,1)} %pad_maximum_fusion), calls=%async_computation.1 | async-start | bytes 10485760 | tf_op jit(solution)/shard_map/all_to_all | solution.py:181
  230.8 3.6 %fusion.96 = f32[256,2048]{1,0:T(8,128)S(1)} fusion(bf16[256,1024]{0,1:T(8,128)(2,1)S(1)} %bitcast.217, bf16[2048,1024]{1,0:T(8,128)(2,1)} %bitcast.8), kind=kOutput, calls=%fused_computation.144 | convolution fusion | flops 1073741824 | bytes 6815744 | tf_op jit(solution)/shard_map/sic,dc->sid/dot_general | solution.py:142
  237.9 63.5 %all-to-all-done.1 = bf16[64,32,1280]{2,1,0:T(8,128)(2,1)} async-done(((bf16[64,32,1280]{2,1,0:T(8,128)(2,1)}), bf16[64,32,1280]{2,1,0:T(8,128)(2,1)}, u32[]{:S(2)}, u32[]{:S(2)}) %all-to-all-start.1) | async-done | bytes 5242912 | tf_op jit(solution)/shard_map/all_to_all | solution.py:181
  301.4 3.4 %convert_reduce_fusion = f32[32,1280]{1,0:T(8,128)S(1)} fusion(bf16[64,32,1280]{2,1,0:T(8,128)(2,1)} %all-to-all-done.1), kind=kLoop, calls=%fused_computation.63 | loop fusion | flops 5201920 | bytes 5406720 | tf_op jit(solution)/shard_map/reduce_sum | solution.py:182
  (150 shorter events, 65.8 us)
Async XLA Ops:
  7.2 42.4 %all-gather.3.cloned.1.call-start = ((), (), s32[]{:S(2)}) async-start(), calls=%async_computation.2 | async-start | bytes 2621440 | tf_op jit(solution)/shard_map/all_gather | solution.py:104
  7.9 103.9 %all-gather.5.cloned.1.call-start = ((), (), s32[]{:S(2)}) async-start(), calls=%async_computation.3 | async-start | bytes 5242880 | tf_op jit(solution)/shard_map/all_gather | solution.py:105
  11.2 77.2 %all-to-all-start = ((bf16[4,512,1024]{2,1,0:T(8,128)(2,1)}), bf16[4,512,1024]{2,1,0:T(8,128)(2,1)}, u32[]{:S(2)}, u32[]{:S(2)}) async-start(bf16[4,512,1024]{2,1,0:T(8,128)(2,1)} %stack.2), calls=%async_computation | async-start | bytes 8388608 | tf_op jit(solution)/shard_map/all_to_all | solution.py:103
  16.7 180.3 %collective-permute-start.10 = (bf16[256,2048]{1,0:T(8,128)(2,1)}, bf16[256,2048]{1,0:T(8,128)(2,1)}, u32[]{:S(2)}, u32[]{:S(2)}) collective-permute-start(bf16[256,2048]{1,0:T(8,128)(2,1)} %bitcast.10), channel_id=1, source_target_pairs={{0,1},{1,0},{2,3},{3,2},{4,5},{5,4},{6,7},{7,6},{8,9},{9,8},{10,11... | collective-permute-start | bytes 3145736 | tf_op jit(solution)/shard_map/ppermute | solution.py:25
  17.5 70.9 %copy-start.11 = (bf16[256,2048]{1,0:T(8,128)(2,1)}, bf16[256,2048]{1,0:T(8,128)(2,1)S(1)}, u32[]{:S(2)}) copy-start(bf16[256,2048]{1,0:T(8,128)(2,1)S(1)} %fusion.78) | copy-start | bytes 3145732
  51.9 40.3 %collective-permute-start = (bf16[1,256,512]{2,1,0:T(8,128)(2,1)S(1)}, bf16[1,256,512]{2,1,0:T(8,128)(2,1)S(1)}, u32[]{:S(2)}, u32[]{:S(2)}) collective-permute-start(bf16[1,256,512]{2,1,0:T(8,128)(2,1)S(1)} %fusion.77), channel_id=1, source_target_pairs={{0,16},{4,20},{8,24},{12,28},{16,32},{20,36},{24,40},{28,44},{32,4... | collective-permute-start | bytes 786440 | tf_op jit(solution)/shard_map/ppermute | solution.py:21
  53.2 43.9 %collective-permute-start.1 = (bf16[1,256,512]{2,1,0:T(8,128)(2,1)S(1)}, bf16[1,256,512]{2,1,0:T(8,128)(2,1)S(1)}, u32[]{:S(2)}, u32[]{:S(2)}) collective-permute-start(bf16[1,256,512]{2,1,0:T(8,128)(2,1)S(1)} %fusion.77), channel_id=1, source_target_pairs={{0,12},{4,16},{8,20},{12,24},{16,28},{20,32},{24,36},{28,40},{32,4... | collective-permute-start | bytes 786440 | tf_op jit(solution)/shard_map/ppermute | solution.py:21
  56.1 41.0 %collective-permute-start.2 = (bf16[1,256,512]{2,1,0:T(8,128)(2,1)S(1)}, bf16[1,256,512]{2,1,0:T(8,128)(2,1)S(1)}, u32[]{:S(2)}, u32[]{:S(2)}) collective-permute-start(bf16[1,256,512]{2,1,0:T(8,128)(2,1)S(1)} %fusion.77), channel_id=1, source_target_pairs={{0,8},{4,12},{8,16},{12,20},{16,24},{20,28},{24,32},{28,36},{32,40... | collective-permute-start | bytes 786440 | tf_op jit(solution)/shard_map/ppermute | solution.py:21
  58.1 50.8 %collective-permute-start.3 = (bf16[1,256,512]{2,1,0:T(8,128)(2,1)S(1)}, bf16[1,256,512]{2,1,0:T(8,128)(2,1)S(1)}, u32[]{:S(2)}, u32[]{:S(2)}) collective-permute-start(bf16[1,256,512]{2,1,0:T(8,128)(2,1)S(1)} %fusion.77), channel_id=1, source_target_pairs={{0,4},{4,8},{8,12},{12,16},{16,20},{20,24},{24,28},{28,32},{32,36}... | collective-permute-start | bytes 786440 | tf_op jit(solution)/shard_map/ppermute | solution.py:21
  118.9 6.0 %copy-start.3 = (bf16[2,1280,128]{2,1,0:T(8,128)(2,1)}, bf16[2,1280,128]{2,1,0:T(8,128)(2,1)S(1)}, u32[]{:S(2)}) copy-start(bf16[2,1280,128]{2,1,0:T(8,128)(2,1)S(1)} %get-tuple-element.280) | copy-start | bytes 1966084 | tf_op jit(solution)/shard_map/while/body/eval_jaxpr/while
  118.9 9.9 %copy-start.5 = (bf16[2,1280,128]{1,2,0:T(8,128)(2,1)}, bf16[2,1280,128]{1,2,0:T(8,128)(2,1)S(1)}, u32[]{:S(2)}) copy-start(bf16[2,1280,128]{1,2,0:T(8,128)(2,1)S(1)} %get-tuple-element.279) | copy-start | bytes 1966084 | tf_op jit(solution)/shard_map/while/body/eval_jaxpr/while
  146.7 6.0 %copy-start.3 = (bf16[2,1280,128]{2,1,0:T(8,128)(2,1)}, bf16[2,1280,128]{2,1,0:T(8,128)(2,1)S(1)}, u32[]{:S(2)}) copy-start(bf16[2,1280,128]{2,1,0:T(8,128)(2,1)S(1)} %get-tuple-element.280) | copy-start | bytes 1966084 | tf_op jit(solution)/shard_map/while/body/eval_jaxpr/while
  146.7 9.9 %copy-start.5 = (bf16[2,1280,128]{1,2,0:T(8,128)(2,1)}, bf16[2,1280,128]{1,2,0:T(8,128)(2,1)S(1)}, u32[]{:S(2)}) copy-start(bf16[2,1280,128]{1,2,0:T(8,128)(2,1)S(1)} %get-tuple-element.279) | copy-start | bytes 1966084 | tf_op jit(solution)/shard_map/while/body/eval_jaxpr/while
  174.6 14.8 %copy-start.16 = (bf16[2,256,4,128]{1,3,2,0:T(8,128)(2,1)S(1)}, bf16[2,256,4,128]{1,3,2,0:T(8,128)(2,1)}, u32[]{:S(2)}) copy-start(bf16[2,256,4,128]{1,3,2,0:T(8,128)(2,1)} %get-tuple-element.83) | copy-start | bytes 1572868
  176.0 13.4 %copy-start.15 = (bf16[2,256,4,128]{1,3,2,0:T(8,128)(2,1)S(1)}, bf16[2,256,4,128]{1,3,2,0:T(8,128)(2,1)}, u32[]{:S(2)}) copy-start(bf16[2,256,4,128]{1,3,2,0:T(8,128)(2,1)} %get-tuple-element.82) | copy-start | bytes 1572868
  176.1 13.4 %collective-permute-start.4 = (bf16[1,256,512]{1,2,0:T(8,128)(2,1)S(1)}, bf16[1,256,512]{1,2,0:T(8,128)(2,1)S(1)}, u32[]{:S(2)}, u32[]{:S(2)}) collective-permute-start(bf16[1,256,512]{1,2,0:T(8,128)(2,1)S(1)} %get-tuple-element.145), channel_id=1, source_target_pairs={{4,0},{8,4},{12,8},{16,12},{20,16},{24,20},{28,24},{32,28},{36,32}... | collective-permute-start | bytes 786440 | tf_op jit(solution)/shard_map/ppermute | solution.py:21
  178.3 16.2 %collective-permute-start.5 = (bf16[1,256,512]{1,2,0:T(8,128)(2,1)S(1)}, bf16[1,256,512]{1,2,0:T(8,128)(2,1)S(1)}, u32[]{:S(2)}, u32[]{:S(2)}) collective-permute-start(bf16[1,256,512]{1,2,0:T(8,128)(2,1)S(1)} %get-tuple-element.148), channel_id=1, source_target_pairs={{8,0},{12,4},{16,8},{20,12},{24,16},{28,20},{32,24},{36,28},{40,32... | collective-permute-start | bytes 786440 | tf_op jit(solution)/shard_map/ppermute | solution.py:21
  180.4 14.1 %collective-permute-start.6 = (bf16[1,256,512]{1,2,0:T(8,128)(2,1)S(1)}, bf16[1,256,512]{1,2,0:T(8,128)(2,1)S(1)}, u32[]{:S(2)}, u32[]{:S(2)}) collective-permute-start(bf16[1,256,512]{1,2,0:T(8,128)(2,1)S(1)} %get-tuple-element.147), channel_id=1, source_target_pairs={{12,0},{16,4},{20,8},{24,12},{28,16},{32,20},{36,24},{40,28},{44,3... | collective-permute-start | bytes 786440 | tf_op jit(solution)/shard_map/ppermute | solution.py:21
  187.4 7.1 %collective-permute-start.7 = (bf16[1,256,512]{1,2,0:T(8,128)(2,1)S(1)}, bf16[1,256,512]{1,2,0:T(8,128)(2,1)S(1)}, u32[]{:S(2)}, u32[]{:S(2)}) collective-permute-start(bf16[1,256,512]{1,2,0:T(8,128)(2,1)S(1)} %get-tuple-element.146), channel_id=1, source_target_pairs={{16,0},{20,4},{24,8},{28,12},{32,16},{36,20},{40,24},{44,28},{48,3... | collective-permute-start | bytes 786440 | tf_op jit(solution)/shard_map/ppermute | solution.py:21
  189.4 7.5 %copy-start.12 = (bf16[256,2048]{1,0:T(8,128)(2,1)S(1)}, bf16[256,2048]{1,0:T(8,128)(2,1)}, u32[]{:S(2)}) copy-start(bf16[256,2048]{1,0:T(8,128)(2,1)} %copy-done.11) | copy-start | bytes 3145732
  194.8 3.9 %collective-permute-start.9 = (bf16[256,1280]{0,1:T(8,128)(2,1)S(1)}, bf16[256,1280]{0,1:T(8,128)(2,1)S(1)}, u32[]{:S(2)}, u32[]{:S(2)}) collective-permute-start(bf16[256,1280]{0,1:T(8,128)(2,1)S(1)} %pad_maximum_fusion.2), channel_id=1, source_target_pairs={{0,1},{1,0},{2,3},{3,2},{4,5},{5,4},{6,7},{7,6},{8,9},{9,8},{10,11... | collective-permute-start | bytes 1966088 | tf_op jit(solution)/shard_map/ppermute | solution.py:25
  196.9 4.7 %collective-permute-start.8 = (bf16[256,2048]{1,0:T(8,128)(2,1)S(1)}, bf16[256,2048]{1,0:T(8,128)(2,1)S(1)}, u32[]{:S(2)}, u32[]{:S(2)}) collective-permute-start(bf16[256,2048]{1,0:T(8,128)(2,1)S(1)} %copy-done.12), channel_id=1, source_target_pairs={{0,1},{1,0},{2,3},{3,2},{4,5},{5,4},{6,7},{7,6},{8,9},{9,8},{10,11... | collective-permute-start | bytes 3145736 | tf_op jit(solution)/shard_map/ppermute | solution.py:25
  206.2 95.2 %all-to-all-start.1 = ((bf16[64,32,1280]{2,1,0:T(8,128)(2,1)}), bf16[64,32,1280]{2,1,0:T(8,128)(2,1)}, u32[]{:S(2)}, u32[]{:S(2)}) async-start(bf16[64,32,1280]{2,1,0:T(8,128)(2,1)} %pad_maximum_fusion), calls=%async_computation.1 | async-start | bytes 10485760 | tf_op jit(solution)/shard_map/all_to_all | solution.py:181
  304.8 3.6 %collective-permute-start.11 = (f32[16,1280]{1,0:T(8,128)S(1)}, f32[16,1280]{1,0:T(8,128)S(1)}, u32[]{:S(2)}, u32[]{:S(2)}) collective-permute-start(f32[16,1280]{1,0:T(8,128)S(1)} %slice_select_fusion), channel_id=1, source_target_pairs={{0,1},{1,0},{2,3},{3,2},{4,5},{5,4},{6,7},{7,6},{8,9},{9,8},{10,11... | collective-permute-start | bytes 245768 | tf_op jit(solution)/shard_map/ppermute | solution.py:25
  (22 other events, 61.5 us)
Sparse Core Ops, SparseCore 0:
  9.7 39.9 all-gather.2
  51.3 60.4 all-gather.4
